TPU v7x, 32 devices: a whole 2x2x4 slice. The times are simulated.
32 devices in a mesh: tensor: 2 (over x), expert: 8 (over z, y), replica: 2 (over core).
Axes of the slice: x: 2, y: 2, z: 4, core: 2. Of those that a mesh axis runs over, the one named last changes fastest.
Arguments:
- tokens: bfloat16 [6304, 768], P(('expert', 'replica')), may hold values from -6 to 6
- gains: float32 [2, 2, 768], replicated, may hold values from 0.5 to 1.5
- attn_qkv: bfloat16 [2, 3, 768, 768], P(None, None, None, 'tensor'), may hold values from -0.21875 to 0.21875
- attn_out: bfloat16 [2, 768, 768], P(None, 'tensor'), may hold values from -3 to 3
- router: bfloat16 [2, 768, 8], replicated, may hold values from -0.15625 to 0.15625
- expert_in: bfloat16 [2, 8, 768, 3072], P(None, 'expert', None, 'tensor'), may hold values from -0.21875 to 0.21875
- expert_out: bfloat16 [2, 8, 3072, 768], P(None, 'expert', 'tensor'), may hold values from -1.75 to 1.75
- routes: int32 [2, 6304, 2], P(None, ('expert', 'replica')), may hold values from 0 to 7, all different within a row; in each aligned block of 394 rows (0 to 393, 394 to 787, ..., all dimensions but the last counted through in order) at most 128 rows name the same one
- cotangent: bfloat16 [6304, 768], P(('expert', 'replica')), may hold values from -6 to 6
Outputs:
- mixed_out: bfloat16 [6304, 768], P(('expert', 'replica'))
- grad_tokens: float32 [6304, 768], P(('expert', 'replica'))
- grad_gains: float32 [2, 2, 768], replicated
- grad_attn_qkv: float32 [2, 3, 768, 768], P(None, None, None, 'tensor')
- grad_attn_out: float32 [2, 768, 768], P(None, 'tensor')
- grad_router: float32 [2, 768, 8], replicated
- grad_expert_in: float32 [2, 8, 768, 3072], P(None, 'expert', 'replica', 'tensor')
- grad_expert_out: float32 [2, 8, 3072, 768], P(None, 'expert', 'tensor', 'replica')
Inputs may be any that keep to these rules, and one draw needn't show every extreme that they name: In the tokens of one block of 394, no expert is named by more than 128 routes, and in every draw some expert by exactly 128; the two experts of a token differ.
All inputs are finite; a program needn't handle non-finite values.
Results may differ from a plain program's by a relative error of at most 0.02.
Values may be sent and summed in bfloat16 or wider, within the bound.
No kernel may reach another device: no remote copies, remote signals or barrier semaphores. Data moves between devices by JAX's collectives and lax.ppermute only.
A program may use at most 192 MiB of HBM per device.

v0:
```python
import jax
import jax.numpy as jnp
from jax import lax
from jax.sharding import PartitionSpec as P

HEAD_DIM = 64
SEQ = 197
EPSILON = 1e-06


def layer_norm(stream, gain):
    center = jnp.mean(stream, axis=-1, keepdims=True)
    shifted = stream - center
    spread = jnp.mean(shifted * shifted, axis=-1, keepdims=True)
    return shifted * lax.rsqrt(spread + EPSILON) * gain


def slot_index(route_ids, expert_count, capacity):
    labels = lax.broadcasted_iota(jnp.int32, (1, 1, expert_count), 2)
    route_hits = jnp.sum((route_ids[:, :, None] == labels).astype(jnp.int32), axis=1)
    before = jnp.cumsum(route_hits, axis=0) - route_hits
    return route_ids * capacity + jnp.take_along_axis(before, route_ids, axis=1)


def on_device(tokens, gains, attn_qkv, attn_out, router, expert_in, expert_out, routes, cotangent):
    row_count, model_width = tokens.shape
    layer_count = attn_qkv.shape[0]
    local_width = attn_qkv.shape[3]
    local_heads = local_width // HEAD_DIM
    image_count = row_count // SEQ
    expert_count = router.shape[2]
    capacity = 8 * (5 * row_count // (16 * expert_count) + 1)
    score_scale = HEAD_DIM ** (-0.5)
    residual = tokens.astype(jnp.float32)
    saved = []
    for layer_index in range(layer_count):
        normed, norm_pull = jax.vjp(layer_norm, residual, gains[layer_index, 0])
        normed_bf = normed.astype(jnp.bfloat16)
        projected = jnp.einsum(
            "td,cdf->ctf", normed_bf, attn_qkv[layer_index], preferred_element_type=jnp.float32
        ).astype(jnp.bfloat16)
        head_view = projected.reshape(3, image_count, SEQ, local_heads, HEAD_DIM)
        scores = (
            jnp.einsum(
                "bqhe,bkhe->bhqk", head_view[0], head_view[1], preferred_element_type=jnp.float32
            )
            * score_scale
        )
        row_max = jnp.max(scores, axis=-1, keepdims=True)
        exp_scores = jnp.exp(scores - row_max)
        exp_total = jnp.sum(exp_scores, axis=-1, keepdims=True)
        log_total = row_max + jnp.log(exp_total)
        attn_probs = (exp_scores / exp_total).astype(jnp.bfloat16)
        mixed_rows = jnp.einsum(
            "bhqk,bkhe->bqhe", attn_probs, head_view[2], preferred_element_type=jnp.float32
        )
        mixed_rows = mixed_rows.reshape(row_count, local_width).astype(jnp.bfloat16)
        attn_part = jnp.dot(mixed_rows, attn_out[layer_index], preferred_element_type=jnp.float32)
        residual = residual + lax.psum(attn_part, "tensor")
        moe_in, moe_pull = jax.vjp(layer_norm, residual, gains[layer_index, 1])
        moe_bf = moe_in.astype(jnp.bfloat16)
        gate_probs = jax.nn.softmax(
            jnp.dot(moe_bf, router[layer_index], preferred_element_type=jnp.float32), axis=-1
        )
        route_ids = routes[layer_index]
        slot_rows = slot_index(route_ids, expert_count, capacity).reshape(-1)
        picked = jnp.take_along_axis(gate_probs, route_ids, axis=1)
        send_buffer = jnp.zeros((expert_count * capacity, model_width), jnp.bfloat16)
        send_buffer = (
            send_buffer.at[slot_rows]
            .set(jnp.repeat(moe_bf, 2, axis=0))
            .reshape(expert_count, capacity, model_width)
        )
        received = lax.all_to_all(send_buffer, "expert", split_axis=0, concat_axis=0, tiled=True)
        source_count = received.shape[0]
        flat_in = received.reshape(-1, model_width)
        pre_act = jnp.dot(flat_in, expert_in[layer_index, 0], preferred_element_type=jnp.float32)
        activation = jax.nn.gelu(pre_act).astype(jnp.bfloat16)
        expert_part = jnp.dot(
            activation, expert_out[layer_index, 0], preferred_element_type=jnp.float32
        )
        expert_part = expert_part.reshape(source_count, capacity, model_width)
        returned = lax.all_to_all(expert_part, "expert", split_axis=0, concat_axis=0, tiled=True)
        chosen = returned.reshape(-1, model_width)[slot_rows].reshape(row_count, 2, model_width)
        moe_part = jnp.sum(picked[:, :, None] * chosen, axis=1)
        residual = residual + lax.psum(moe_part, "tensor")
        kept_act = pre_act
        saved.append(
            (
                normed_bf,
                norm_pull,
                head_view,
                log_total,
                mixed_rows,
                moe_bf,
                moe_pull,
                gate_probs,
                route_ids,
                slot_rows,
                picked,
                received,
                kept_act,
                chosen,
            )
        )
    mixed_out = residual.astype(jnp.bfloat16)
    upstream = cotangent.astype(jnp.float32)
    raw_grads = [None] * layer_count
    labels = lax.broadcasted_iota(jnp.int32, (1, 1, expert_count), 2)
    for layer_index in reversed(range(layer_count)):
        (
            normed_bf,
            norm_pull,
            head_view,
            log_total,
            mixed_rows,
            moe_bf,
            moe_pull,
            gate_probs,
            route_ids,
            slot_rows,
            picked,
            received,
            kept_act,
            chosen,
        ) = saved[layer_index]
        slot_grad = (
            (picked[:, :, None] * upstream[:, None, :])
            .astype(jnp.bfloat16)
            .reshape(-1, model_width)
        )
        grad_send = jnp.zeros((expert_count * capacity, model_width), jnp.bfloat16)
        grad_send = (
            grad_send.at[slot_rows].set(slot_grad).reshape(expert_count, capacity, model_width)
        )
        grad_recv = lax.all_to_all(grad_send, "expert", split_axis=0, concat_axis=0, tiled=True)
        source_count = grad_recv.shape[0]
        grad_recv = grad_recv.reshape(-1, model_width)
        flat_in = received.reshape(-1, model_width)
        pre_act = kept_act
        activation, gelu_pull = jax.vjp(jax.nn.gelu, pre_act)
        act_grad = jnp.einsum(
            "sd,fd->sf", grad_recv, expert_out[layer_index, 0], preferred_element_type=jnp.float32
        )
        pre_grad = gelu_pull(act_grad)[0].astype(jnp.bfloat16)
        grad_w_out = jnp.einsum(
            "sf,sd->fd",
            activation.astype(jnp.bfloat16),
            grad_recv,
            preferred_element_type=jnp.float32,
        )
        grad_w_in = jnp.einsum("sd,sf->df", flat_in, pre_grad, preferred_element_type=jnp.float32)
        input_grad = jnp.einsum(
            "sf,df->sd", pre_grad, expert_in[layer_index, 0], preferred_element_type=jnp.float32
        )
        input_grad = input_grad.reshape(source_count, capacity, model_width)
        home_grad = lax.all_to_all(input_grad, "expert", split_axis=0, concat_axis=0, tiled=True)
        row_grad = jnp.sum(
            home_grad.reshape(-1, model_width)[slot_rows].reshape(row_count, 2, model_width), axis=1
        )
        gate_dot = jnp.sum(upstream[:, None, :] * chosen, axis=-1)
        row_grad, gate_dot = lax.psum((row_grad, gate_dot), "tensor")
        prob_grad = jnp.sum(
            gate_dot[:, :, None] * (route_ids[:, :, None] == labels).astype(jnp.float32), axis=1
        )
        logit_grad = gate_probs * (
            prob_grad - jnp.sum(prob_grad * gate_probs, axis=-1, keepdims=True)
        )
        logit_grad = logit_grad.astype(jnp.bfloat16)
        grad_router = jnp.einsum(
            "td,te->de", moe_bf, logit_grad, preferred_element_type=jnp.float32
        )
        norm_grad = row_grad + jnp.einsum(
            "te,de->td", logit_grad, router[layer_index], preferred_element_type=jnp.float32
        )
        resid_grad, gain_two = moe_pull(norm_grad)
        upstream = upstream + resid_grad
        out_grad = upstream.astype(jnp.bfloat16)
        grad_attn_out = jnp.einsum(
            "tf,td->fd", mixed_rows, out_grad, preferred_element_type=jnp.float32
        )
        mixed_grad = jnp.einsum(
            "td,fd->tf", out_grad, attn_out[layer_index], preferred_element_type=jnp.float32
        )
        mixed_grad = mixed_grad.astype(jnp.bfloat16).reshape(
            image_count, SEQ, local_heads, HEAD_DIM
        )
        scores = (
            jnp.einsum(
                "bqhe,bkhe->bhqk", head_view[0], head_view[1], preferred_element_type=jnp.float32
            )
            * score_scale
        )
        attn_probs = jnp.exp(scores - log_total)
        value_grad = jnp.einsum(
            "bhqk,bqhe->bkhe",
            attn_probs.astype(jnp.bfloat16),
            mixed_grad,
            preferred_element_type=jnp.float32,
        )
        prob_grad = jnp.einsum(
            "bqhe,bkhe->bhqk", mixed_grad, head_view[2], preferred_element_type=jnp.float32
        )
        score_grad = attn_probs * (
            prob_grad - jnp.sum(prob_grad * attn_probs, axis=-1, keepdims=True)
        )
        score_grad = score_grad.astype(jnp.bfloat16)
        query_grad = (
            jnp.einsum(
                "bhqk,bkhe->bqhe", score_grad, head_view[1], preferred_element_type=jnp.float32
            )
            * score_scale
        )
        key_grad = (
            jnp.einsum(
                "bhqk,bqhe->bkhe", score_grad, head_view[0], preferred_element_type=jnp.float32
            )
            * score_scale
        )
        proj_grad = (
            jnp.stack([query_grad, key_grad, value_grad])
            .reshape(3, row_count, local_width)
            .astype(jnp.bfloat16)
        )
        grad_qkv = jnp.einsum(
            "td,ctf->cdf", normed_bf, proj_grad, preferred_element_type=jnp.float32
        )
        norm_grad = jnp.einsum(
            "ctf,cdf->td", proj_grad, attn_qkv[layer_index], preferred_element_type=jnp.float32
        )
        norm_grad = lax.psum(norm_grad, "tensor")
        resid_grad, gain_one = norm_pull(norm_grad)
        upstream = upstream + resid_grad
        gain_pair = jnp.stack([gain_one, gain_two])
        raw_grads[layer_index] = (
            grad_w_in,
            grad_w_out,
            grad_qkv,
            grad_attn_out,
            grad_router,
            gain_pair,
        )
    stacked = [jnp.stack([item[position] for item in raw_grads]) for position in range(6)]
    grad_in_all, grad_out_all = (
        lax.psum_scatter(stacked[0], "replica", scatter_dimension=1, tiled=True),
        lax.psum_scatter(stacked[1], "replica", scatter_dimension=2, tiled=True),
    )
    grad_qkv_all, grad_proj_all, grad_router_all, grad_gain_all = lax.psum(
        (stacked[2], stacked[3], stacked[4], stacked[5]), ("expert", "replica")
    )
    return (
        mixed_out,
        upstream,
        grad_gain_all,
        grad_qkv_all,
        grad_proj_all,
        grad_router_all,
        grad_in_all[:, None],
        grad_out_all[:, None],
    )


def solution(mesh):
    return jax.shard_map(
        on_device,
        mesh=mesh,
        in_specs=(
            P(("expert", "replica"), None),
            P(),
            P(None, None, None, "tensor"),
            P(None, "tensor", None),
            P(),
            P(None, "expert", None, "tensor"),
            P(None, "expert", "tensor", None),
            P(None, ("expert", "replica"), None),
            P(("expert", "replica"), None),
        ),
        out_specs=(
            P(("expert", "replica"), None),
            P(("expert", "replica"), None),
            P(),
            P(None, None, None, "tensor"),
            P(None, "tensor", None),
            P(),
            P(None, "expert", "replica", "tensor"),
            P(None, "expert", "tensor", "replica"),
        ),
        check_vma=False,
    )
```

profile of v0, /device:TPU:0, one launch (start us, length us, event | category | flops | bytes accessed | tf_op | source)
XLA Modules:
  0.0 1209.6 jit_solution(15359523138905654827)
XLA Ops:
  24.5 8.1 gather_fusion.5
  33.1 35.5 %all-reduce.14.cloned.1.call-done = f32[394,768]{1,0:T(8,128)} async-done(((f32[394,768]{1,0:T(8,128)}), f32[394,768]{1,0:T(8,128)}) %all-reduce.14.cloned.1.call-update) | async-done | bytes 1210384 | tf_op jit(solution)/shard_map/psum | solution.py:59
  73.3 6.1 scatter_custom_fusion
  79.4 42.6 %all_to_all.40 = bf16[8,128,768]{2,1,0:T(8,128)(2,1)S(1)} all-to-all(bf16[8,128,768]{2,1,0:T(8,128)(2,1)S(1)} %bitcast.271), channel_id=1, replica_groups=mesh['tensor'=2,'expert'=8,'replica'=2] {'expert'}, dimensions={0} | all-to-all | bytes 3145728 | tf_op jit(solution)/shard_map/all_to_all | solution.py:74
  122.0 7.6 multiply_convert_fusion.1
  129.6 4.3 fusion.20
  133.9 3.8 all-to-all-start.1
  139.7 8.3 gather_fusion.4
  150.6 57.4 %all-to-all-done.1 = f32[8,128,768]{2,1,0:T(8,128)S(1)} async-done(((f32[8,128,768]{2,1,0:T(8,128)}), f32[8,128,768]{2,1,0:T(8,128)S(1)}, u32[]{:S(2)}, u32[]{:S(2)}) %all-to-all-start.1) | async-done | bytes 3145760 | tf_op jit(solution)/shard_map/all_to_all | solution.py:83
  208.0 3.8 gather_fusion
  211.8 3.1 reshape.413
  216.3 3.9 multiply_reduce_fusion.5
  221.5 41.1 %all-reduce.16.cloned.1.call-done = f32[394,768]{1,0:T(8,128)} async-done(((f32[394,768]{1,0:T(8,128)}), f32[394,768]{1,0:T(8,128)}) %all-reduce.16.cloned.1.call-update) | async-done | bytes 1210384 | tf_op jit(solution)/shard_map/psum | solution.py:86
  279.7 8.1 gather_fusion.7
  288.3 33.4 %all-reduce.18.cloned.1.call-done = f32[394,768]{1,0:T(8,128)} async-done(((f32[394,768]{1,0:T(8,128)}), f32[394,768]{1,0:T(8,128)}) %all-reduce.18.cloned.1.call-update) | async-done | bytes 1210384 | tf_op jit(solution)/shard_map/psum | solution.py:59
  326.6 7.5 scatter_custom_fusion.1
  334.1 5.8 all-to-all-start.2
  342.0 4.1 mul.501
  346.4 8.1 gather_fusion.6
  355.0 10.8 scatter_custom_fusion.2
  365.7 11.1 all-to-all-done.2
  376.9 4.5 all-to-all-start.4
  381.4 7.5 multiply_convert_fusion
  388.9 29.1 %all-to-all-done.4 = bf16[8,128,768]{2,1,0:T(8,128)(2,1)} async-done(((bf16[8,128,768]{2,1,0:T(8,128)(2,1)}), bf16[8,128,768]{2,1,0:T(8,128)(2,1)}, u32[]{:S(2)}, u32[]{:S(2)}) %all-to-all-start.4) | async-done | bytes 1572896 | tf_op jit(solution)/shard_map/all_to_all | solution.py:136
  418.0 8.5 fusion.13
  428.2 4.3 fusion.16
  432.5 3.7 all-to-all-start.5
  436.1 6.9 fusion.18
  443.0 64.0 %all-to-all-done.5 = f32[8,128,768]{2,1,0:T(8,128)S(1)} async-done(((f32[8,128,768]{2,1,0:T(8,128)}), f32[8,128,768]{2,1,0:T(8,128)S(1)}, u32[]{:S(2)}, u32[]{:S(2)}) %all-to-all-start.5) | async-done | bytes 3145760 | tf_op jit(solution)/shard_map/all_to_all | solution.py:157
  508.7 3.6 all-to-all-start.3
  512.4 6.9 gather_fusion.2
  519.2 4.0 reshape.425
  523.2 5.6 reduce_sum.406
  531.1 52.1 %all-to-all-done.3 = f32[8,128,768]{2,1,0:T(8,128)S(1)} async-done(((f32[8,128,768]{2,1,0:T(8,128)}), f32[8,128,768]{2,1,0:T(8,128)S(1)}, u32[]{:S(2)}, u32[]{:S(2)}) %all-to-all-start.3) | async-done | bytes 3145760 | tf_op jit(solution)/shard_map/all_to_all | solution.py:83
  583.2 3.8 gather_fusion.1
  587.0 4.1 reshape.421
  591.1 8.1 multiply_reduce_fusion.3
  599.2 9.9 psum.103
  625.0 3.5 fusion.71
  629.0 42.9 %all-reduce.22.cloned.1.call-done = f32[394,768]{1,0:T(8,128)} async-done(((f32[394,768]{1,0:T(8,128)}), f32[394,768]{1,0:T(8,128)}) %all-reduce.22.cloned.1.call-update) | async-done | bytes 1210384 | tf_op jit(solution)/shard_map/psum | solution.py:231
  678.7 3.2 mul.539
  681.9 8.9 scatter_custom_fusion.3
  690.8 42.5 %all_to_all.41 = bf16[8,128,768]{2,1,0:T(8,128)(2,1)S(1)} all-to-all(bf16[8,128,768]{2,1,0:T(8,128)(2,1)} %bitcast.270), channel_id=1, replica_groups=mesh['tensor'=2,'expert'=8,'replica'=2] {'expert'}, dimensions={0} | all-to-all | bytes 3145728 | tf_op jit(solution)/shard_map/all_to_all | solution.py:136
  733.3 9.1 fusion.6
  745.1 74.1 %all_to_all.42 = f32[8,128,768]{2,1,0:T(8,128)S(1)} all-to-all(f32[8,128,768]{2,1,0:T(8,128)S(1)} %fusion.14), channel_id=1, replica_groups=mesh['tensor'=2,'expert'=8,'replica'=2] {'expert'}, dimensions={0} | all-to-all | bytes 6291456 | tf_op jit(solution)/shard_map/all_to_all | solution.py:157
  819.2 3.8 gather_fusion.3
  823.0 4.0 reshape.430
  827.0 5.7 reduce_sum.415
  832.9 3.1 multiply_reduce_fusion.2
  836.0 14.5 %psum.106 = f32[394,2]{1,0:T(8,128)S(1)} all-reduce(f32[394,2]{1,0:T(8,128)S(1)} %multiply_reduce_fusion.2), channel_id=1, replica_groups=mesh['tensor'=2,'expert'=8,'replica'=2] {'tensor'}, use_global_device_ids=true, to_apply=%region_47.50 | all-reduce | flops 788 | bytes 6304 | tf_op jit(solution)/shard_map/psum | solution.py:162
  850.8 27.6 %all-reduce.24.cloned.1.call-done = f32[394,768]{1,0:T(8,128)} async-done(((f32[394,768]{1,0:T(8,128)}), f32[394,768]{1,0:T(8,128)}) %all-reduce.24.cloned.1.call-update) | async-done | bytes 1210384 | tf_op jit(solution)/shard_map/psum | solution.py:162
  893.2 3.9 fusion.68
  905.3 3.4 pad_maximum_fusion.2
  908.9 5.2 convolution_bitcast_fusion
  916.9 4.2 pad_maximum_fusion.1
  921.4 5.2 convolution_bitcast_fusion.2
  929.3 4.5 pad_maximum_fusion
  935.3 32.9 %all-reduce.28.cloned.1.call-done = (f32[394,768]{1,0:T(8,128)}, f32[394,768]{1,0:T(8,128)}) async-done(((f32[394,768]{1,0:T(8,128)}, f32[394,768]{1,0:T(8,128)}), (f32[394,768]{1,0:T(8,128)}, f32[394,768]{1,0:T(8,128)})) %all-reduce.28.cloned.1.call-update) | async-done | bytes 2420752 | tf_op jit(solution)/shard_map/psum | solution.py:86
  970.7 65.3 %all-reduce.2 = (f32[2,2,768]{2,1,0:T(2,128)}, f32[2,768,8]{1,2,0:T(8,128)}) all-reduce(f32[2,2,768]{2,1,0:T(2,128)S(1)} %pad_maximum_fusion.5, f32[2,768,8]{1,2,0:T(8,128)S(1)} %pad_maximum_fusion.4), channel_id=1, replica_groups=mesh['tensor'=2,'expert'=8,'replica'=2] {'expert','replica'}, use_global_device_ids=true, to_apply=%region_60.63 | all-reduce | flops 15360 | bytes 122880 | tf_op jit(solution)/shard_map/psum | solution.py:248
  1036.0 3.4 add_add_fusion.4
  1039.5 118.8 %all-reduce.26.cloned.1.call-done = (f32[2,3,768,384]{2,3,1,0:T(8,128)}, f32[2,384,768]{2,1,0:T(8,128)}) async-done(((f32[2,3,768,384]{2,3,1,0:T(8,128)}, f32[2,384,768]{2,1,0:T(8,128)}), (f32[2,3,768,384]{2,3,1,0:T(8,128)}, f32[2,384,768]{2,1,0:T(8,128)})) %all-reduce.26.cloned.1.call-update) | async-done | bytes 9437200 | tf_op jit(solution)/shard_map/psum | solution.py:248
  1158.3 8.2 copy.267
  1166.5 12.7 %reduce-scatter.5.cloned.1.call-done = f32[2,1536,384]{2,1,0:T(8,128)} async-done(((f32[2,1536,768]{2,1,0:T(8,128)}), f32[2,1536,384]{2,1,0:T(8,128)}) %reduce-scatter.5.cloned.1.call-update) | async-done | bytes 4718608 | tf_op jit(solution)/shard_map/reduce_scatter | solution.py:246
  1179.1 22.0 %reduce-scatter.3.cloned.1.call-done = f32[2,384,1536]{2,1,0:T(8,128)} async-done(((f32[2,768,1536]{2,1,0:T(8,128)}), f32[2,384,1536]{2,1,0:T(8,128)}) %reduce-scatter.3.cloned.1.call-update) | async-done | bytes 4718608 | tf_op jit(solution)/shard_map/reduce_scatter | solution.py:245
  (459 shorter events, 119.6 us)
Async XLA Ops:
  7.2 61.4 %all-reduce.14.cloned.1.call-start = ((), (), s32[]{:S(2)}) async-start(), calls=%async_computation.10 | async-start | bytes 2457600 | tf_op jit(solution)/shard_map/psum | solution.py:59
  8.5 5.6 copy-start.94
  11.3 59.1 %copy-start.85 = (f32[768]{0:T(1024)}, f32[768]{0:T(1024)S(1)}, u32[]{:S(2)}) copy-start(f32[768]{0:T(1024)S(1)} %get-tuple-element.61) | copy-start | bytes 9220
  24.5 44.1 %copy-start.14 = (bf16[394,768]{1,0:T(8,128)(2,1)S(1)}, bf16[394,768]{1,0:T(8,128)(2,1)}, u32[]{:S(2)}) copy-start(bf16[394,768]{1,0:T(8,128)(2,1)} %param.13) | copy-start | bytes 1815556
  33.1 104.6 %copy-start.116 = (s32[788]{0:T(1024)}, s32[788]{0:T(1024)S(1)}, u32[]{:S(2)}) copy-start(s32[788]{0:T(1024)S(1)} %fusion.150) | copy-start | bytes 9460
  79.4 50.2 %slice-start = ((s8[4718592]{0:T(1024)(128)(4,1)}), s8[4194304]{0:T(1024)(128)(4,1)S(1)}, s32[]{:S(2)}) async-start(s8[4718592]{0:T(1024)(128)(4,1)} %bitcast.280), calls=%async_computation.20 | async-start | bytes 8388608
  122.0 7.6 copy-start.32
  122.0 7.6 slice-start.1
  133.9 74.1 %all-to-all-start.1 = ((f32[8,128,768]{2,1,0:T(8,128)}), f32[8,128,768]{2,1,0:T(8,128)S(1)}, u32[]{:S(2)}, u32[]{:S(2)}) async-start(f32[8,128,768]{2,1,0:T(8,128)} %fusion.20), calls=%async_computation.1 | async-start | bytes 6291456 | tf_op jit(solution)/shard_map/all_to_all | solution.py:83
  137.7 124.9 %all-reduce.16.cloned.1.call-start = ((), (), s32[]{:S(2)}) async-start(), calls=%async_computation.11 | async-start | bytes 2457600 | tf_op jit(solution)/shard_map/psum | solution.py:86
  137.7 70.2 %copy-start.100 = (s32[1024]{0:T(1024)}, s32[1024]{0:T(1024)S(1)}, u32[]{:S(2)}) copy-start(s32[1024]{0:T(1024)S(1)} %pad_clamp_fusion.1) | copy-start | bytes 12292
  139.7 8.4 copy-start.106
  220.3 42.3 %copy-start.9 = (f32[394,768]{1,0:T(8,128)S(1)}, f32[394,768]{1,0:T(8,128)}, u32[]{:S(2)}) copy-start(f32[394,768]{1,0:T(8,128)} %copy-done.8) | copy-start | bytes 3631108
  220.3 101.4 %all-reduce.18.cloned.1.call-start = ((), (), s32[]{:S(2)}) async-start(), calls=%async_computation.12 | async-start | bytes 2457600 | tf_op jit(solution)/shard_map/psum | solution.py:59
  221.5 43.1 %copy-start.83 = (f32[768]{0:T(1024)S(1)}, f32[768]{0:T(1024)}, u32[]{:S(2)}) copy-start(f32[768]{0:T(1024)} %get-tuple-element.63) | copy-start | bytes 9220
  264.2 57.4 %copy-start.11 = (f32[394,768]{1,0:T(8,128)}, f32[394,768]{1,0:T(8,128)S(1)}, u32[]{:S(2)}) copy-start(f32[394,768]{1,0:T(8,128)S(1)} %get-tuple-element.79) | copy-start | bytes 3631108
  267.0 5.7 copy-start.45
  288.3 36.0 %copy-start.87 = (f32[768]{0:T(1024)S(1)}, f32[768]{0:T(1024)}, u32[]{:S(2)}) copy-start(f32[768]{0:T(1024)} %get-tuple-element.60) | copy-start | bytes 9220
  324.4 21.6 %copy-start.30 = (bf16[394,768]{1,0:T(8,128)(2,1)}, bf16[394,768]{1,0:T(8,128)(2,1)S(1)}, u32[]{:S(2)}) copy-start(bf16[394,768]{1,0:T(8,128)(2,1)S(1)} %multiply_convert_fusion.6) | copy-start | bytes 1815556
  334.1 5.9 copy-start.24
  334.1 42.8 %all-to-all-start.2 = ((bf16[8,128,768]{2,1,0:T(8,128)(2,1)}), bf16[8,128,768]{2,1,0:T(8,128)(2,1)S(1)}, u32[]{:S(2)}, u32[]{:S(2)}) async-start(bf16[8,128,768]{2,1,0:T(8,128)(2,1)} %bitcast.268), calls=%async_computation.2 | async-start | bytes 3145728 | tf_op jit(solution)/shard_map/all_to_all | solution.py:74
  376.9 12.0 copy-start.34
  376.9 41.2 %all-to-all-start.4 = ((bf16[8,128,768]{2,1,0:T(8,128)(2,1)}), bf16[8,128,768]{2,1,0:T(8,128)(2,1)}, u32[]{:S(2)}, u32[]{:S(2)}) async-start(bf16[8,128,768]{2,1,0:T(8,128)(2,1)} %bitcast.269), calls=%async_computation.4 | async-start | bytes 3145728 | tf_op jit(solution)/shard_map/all_to_all | solution.py:136
  381.4 46.8 %slice-start.2 = ((s8[4718592]{0:T(1024)(128)(4,1)}), s8[524288]{0:T(1024)(128)(4,1)S(1)}, s32[]{:S(2)}) async-start(s8[4718592]{0:T(1024)(128)(4,1)} %bitcast.282), calls=%async_computation.22 | async-start | bytes 1048576
  418.0 10.1 slice-start.3
  432.5 74.5 %all-to-all-start.5 = ((f32[8,128,768]{2,1,0:T(8,128)}), f32[8,128,768]{2,1,0:T(8,128)S(1)}, u32[]{:S(2)}, u32[]{:S(2)}) async-start(f32[8,128,768]{2,1,0:T(8,128)} %fusion.16), calls=%async_computation.5 | async-start | bytes 6291456 | tf_op jit(solution)/shard_map/all_to_all | solution.py:157
  508.7 74.5 %all-to-all-start.3 = ((f32[8,128,768]{2,1,0:T(8,128)}), f32[8,128,768]{2,1,0:T(8,128)S(1)}, u32[]{:S(2)}, u32[]{:S(2)}) async-start(f32[8,128,768]{2,1,0:T(8,128)} %fusion.18), calls=%async_computation.3 | async-start | bytes 6291456 | tf_op jit(solution)/shard_map/all_to_all | solution.py:83
  512.3 97.0 %all-reduce.20.cloned.1.call-start = ((), (), s32[]{:S(2)}) async-start(), calls=%async_computation.13 | async-start | bytes 2457600 | tf_op jit(solution)/shard_map/psum | solution.py:162
  528.9 143.0 %all-reduce.22.cloned.1.call-start = ((), (), s32[]{:S(2)}) async-start(), calls=%async_computation.14 | async-start | bytes 2457600 | tf_op jit(solution)/shard_map/psum | solution.py:231
  591.1 18.1 %copy-start.99 = (s32[394,2]{0,1:T(2,128)S(1)}, s32[394,2]{0,1:T(2,128)}, u32[]{:S(2)}) copy-start(s32[394,2]{0,1:T(2,128)} %copy-done.98) | copy-start | bytes 9460
  591.1 18.2 %copy-start.6 = (f32[394,768]{1,0:T(8,128)S(1)}, f32[394,768]{1,0:T(8,128)}, u32[]{:S(2)}) copy-start(f32[394,768]{1,0:T(8,128)} %copy-done.5) | copy-start | bytes 3631108
  625.0 46.9 %copy-start.84 = (f32[768]{0:T(1024)S(1)}, f32[768]{0:T(1024)}, u32[]{:S(2)}) copy-start(f32[768]{0:T(1024)} %get-tuple-element.63) | copy-start | bytes 9220
  625.0 46.9 %copy-start.89 = (f32[394]{0:T(512)S(1)}, f32[394]{0:T(512)}, u32[]{:S(2)}) copy-start(f32[394]{0:T(512)} %copy-done.88) | copy-start | bytes 4732
  625.0 46.9 %copy-start.103 = (f32[394]{0:T(512)S(1)}, f32[394]{0:T(512)}, u32[]{:S(2)}) copy-start(f32[394]{0:T(512)} %copy-done.102) | copy-start | bytes 4732
  628.6 43.3 %copy-start.12 = (f32[394,768]{1,0:T(8,128)S(1)}, f32[394,768]{1,0:T(8,128)}, u32[]{:S(2)}) copy-start(f32[394,768]{1,0:T(8,128)} %copy-done.11) | copy-start | bytes 3631108
  628.6 45.2 %copy-start.113 = (f32[394]{0:T(512)S(1)}, f32[394]{0:T(512)}, u32[]{:S(2)}) copy-start(f32[394]{0:T(512)} %copy-done.112) | copy-start | bytes 4732
  628.6 249.8 %all-reduce.24.cloned.1.call-start = ((), (), s32[]{:S(2)}) async-start(), calls=%async_computation.15 | async-start | bytes 2457600 | tf_op jit(solution)/shard_map/psum | solution.py:162
  681.9 60.6 %slice-start.4 = ((s8[4718592]{0:T(1024)(128)(4,1)}), s8[524288]{0:T(1024)(128)(4,1)S(1)}, s32[]{:S(2)}) async-start(s8[4718592]{0:T(1024)(128)(4,1)} %bitcast.284), calls=%async_computation.24 | async-start | bytes 1048576
  733.3 9.1 copy-start.61
  733.3 9.1 slice-start.5
  745.1 74.1 %copy-start.101 = (s32[1024]{0:T(1024)S(1)}, s32[1024]{0:T(1024)}, u32[]{:S(2)}) copy-start(s32[1024]{0:T(1024)} %copy-done.100) | copy-start | bytes 12292
  827.0 5.8 copy-start.71
  827.0 5.8 copy-start.80
  827.0 5.8 copy-start.18
  832.7 135.4 %all-reduce.28.cloned.1.call-start = ((), (), s32[]{:S(2)}) async-start(), calls=%async_computation.19 | async-start | bytes 4915200 | tf_op jit(solution)/shard_map/psum | solution.py:86
  832.8 17.8 %copy-start.97 = (s32[394,2]{0,1:T(2,128)S(1)}, s32[394,2]{0,1:T(2,128)}, u32[]{:S(2)}) copy-start(s32[394,2]{0,1:T(2,128)} %copy-done.96) | copy-start | bytes 9460
  832.9 17.8 %copy-start.69 = (f32[394,8]{0,1:T(8,128)S(1)}, f32[394,8]{0,1:T(8,128)}, u32[]{:S(2)}) copy-start(f32[394,8]{0,1:T(8,128)} %copy-done.68) | copy-start | bytes 37828
  832.9 17.8 %copy-start.93 = (f32[394]{0:T(512)S(1)}, f32[394]{0:T(512)}, u32[]{:S(2)}) copy-start(f32[394]{0:T(512)} %copy-done.92) | copy-start | bytes 4732
  832.9 17.8 %copy-start.107 = (f32[394]{0:T(512)S(1)}, f32[394]{0:T(512)}, u32[]{:S(2)}) copy-start(f32[394]{0:T(512)} %copy-done.106) | copy-start | bytes 4732
  832.9 45.5 %copy-start.10 = (f32[394,768]{1,0:T(8,128)S(1)}, f32[394,768]{1,0:T(8,128)}, u32[]{:S(2)}) copy-start(f32[394,768]{1,0:T(8,128)} %copy-done.8) | copy-start | bytes 3631108
  832.9 45.5 %copy-start.86 = (f32[768]{0:T(1024)S(1)}, f32[768]{0:T(1024)}, u32[]{:S(2)}) copy-start(f32[768]{0:T(1024)} %copy-done.85) | copy-start | bytes 9220
  832.9 45.5 %copy-start.91 = (f32[394]{0:T(512)S(1)}, f32[394]{0:T(512)}, u32[]{:S(2)}) copy-start(f32[394]{0:T(512)} %copy-done.90) | copy-start | bytes 4732
  832.9 45.5 %copy-start.105 = (f32[394]{0:T(512)S(1)}, f32[394]{0:T(512)}, u32[]{:S(2)}) copy-start(f32[394]{0:T(512)} %copy-done.104) | copy-start | bytes 4732
  850.8 29.5 %copy-start.111 = (f32[394]{0:T(512)S(1)}, f32[394]{0:T(512)}, u32[]{:S(2)}) copy-start(f32[394]{0:T(512)} %copy-done.110) | copy-start | bytes 4732
  897.1 261.2 %all-reduce.26.cloned.1.call-start = ((), (), s32[]{:S(2)}) async-start(), calls=%async_computation.18 | async-start | bytes 18874368 | tf_op jit(solution)/shard_map/psum | solution.py:248
  908.8 5.3 copy-start.62
  908.8 270.3 %reduce-scatter.5.cloned.1.call-start = ((), (), s32[]{:S(2)}) async-start(), calls=%async_computation.17 | async-start | bytes 14155776 | tf_op jit(solution)/shard_map/reduce_scatter | solution.py:246
  908.8 5.3 copy-start.120
  921.2 5.5 copy-start.33
  921.2 280.0 %reduce-scatter.3.cloned.1.call-start = ((), (), s32[]{:S(2)}) async-start(), calls=%async_computation.16 | async-start | bytes 14155776 | tf_op jit(solution)/shard_map/reduce_scatter | solution.py:245
  921.4 5.2 copy-start.55
  934.9 35.1 %copy-start.109 = (f32[394]{0:T(512)S(1)}, f32[394]{0:T(512)}, u32[]{:S(2)}) copy-start(f32[394]{0:T(512)} %copy-done.108) | copy-start | bytes 4732
  968.2 67.8 %copy-start.7 = (f32[394,768]{1,0:T(8,128)S(1)}, f32[394,768]{1,0:T(8,128)}, u32[]{:S(2)}) copy-start(f32[394,768]{1,0:T(8,128)} %copy-done.5) | copy-start | bytes 3631108
  1158.3 42.9 %copy-start.56 = (f32[2,384,768]{2,1,0:T(8,128)S(1)}, f32[2,384,768]{2,1,0:T(8,128)}, u32[]{:S(2)}) copy-start(f32[2,384,768]{2,1,0:T(8,128)} %get-tuple-element.116) | copy-start | bytes 7077892
  (78 other events, 137.3 us)
Sparse Core Ops, SparseCore 0:
  21.9 46.6 all-reduce.13
  220.4 42.0 all-reduce.15
  277.6 43.9 all-reduce.17
  529.0 44.3 all-reduce.19
  628.7 43.1 all-reduce.21
  832.9 45.4 all-reduce.23
  897.2 70.9 all-reduce.27
  972.5 185.7 all-reduce.25
  1161.2 17.8 reduce-scatter.4
  1181.9 19.1 reduce-scatter.2
where the time goes:
time: 1220 us; the launch traced here: 1210 us
  waiting for transfers between devices  581 us (48%)
  blocking collectives  249 us (20%)
  local copies, waits for them, and re-layouts  154 us (13%)
  matrix products  98.9 us (8%)
  other arithmetic  88.1 us (7%)
  starting transfers between devices  22.7 us (2%)
  between operations  16.4 us (1%)
    psum x1, waiting for transfers between devices, on_device(): lax.psum((stacked[2], stacked[3], stacked[4], stacked[5]), ('expert', 're...  119 us
    all_to_all x2, waiting for transfers between devices, on_device(): lax.all_to_all(expert_part, 'expert', split_axis=0, concat_axis=0, tiled=...  109 us
    all_to_all x1, blocking collectives, on_device(): lax.all_to_all(input_grad, 'expert', split_axis=0, concat_axis=0, tiled=T...  74.1 us
    psum x2, waiting for transfers between devices, on_device(): residual = residual + lax.psum(moe_part, 'tensor')  74 us
    psum x2, waiting for transfers between devices, on_device(): residual = residual + lax.psum(attn_part, 'tensor')  68.9 us
    psum x1, blocking collectives, on_device(): lax.psum((stacked[2], stacked[3], stacked[4], stacked[5]), ('expert', 're...  65.3 us
    all_to_all x1, waiting for transfers between devices, on_device(): lax.all_to_all(input_grad, 'expert', split_axis=0, concat_axis=0, tiled=T...  64 us
    psum x1, waiting for transfers between devices, on_device(): norm_grad = lax.psum(norm_grad, 'tensor')  42.9 us
  transfers between devices with their start and end apart: 15, of which 14 were waited for; matrix products, arithmetic and copies ran while one was open for 13% of the time, Pallas kernels for 0%

commit v1 on v0

--- a/solution.py
+++ b/solution.py
@@ -71,7 +71,19 @@
             .set(jnp.repeat(moe_bf, 2, axis=0))
             .reshape(expert_count, capacity, model_width)
         )
-        received = lax.all_to_all(send_buffer, "expert", split_axis=0, concat_axis=0, tiled=True)
+        ways, here = (lax.axis_size("expert"), lax.axis_index("expert"))
+        width = send_buffer.shape[0] // ways
+        shape = list(send_buffer.shape)
+        shape[0] = width
+        height = shape[0]
+        shape[0] = height * ways
+        full = jnp.zeros(shape, send_buffer.dtype)
+        for mask in range(ways):
+            part = lax.dynamic_slice_in_dim(send_buffer, (here ^ mask) * width, width, axis=0)
+            if mask:
+                part = lax.ppermute(part, "expert", [(d, d ^ mask) for d in range(ways)])
+            full = lax.dynamic_update_slice_in_dim(full, part, (here ^ mask) * height, axis=0)
+        received = full
         source_count = received.shape[0]
         flat_in = received.reshape(-1, model_width)
         pre_act = jnp.dot(flat_in, expert_in[layer_index, 0], preferred_element_type=jnp.float32)

time: 1220 us -> 1220 us (level)
  blocking collectives: 249 us -> 206 us
  waiting for transfers between devices: 581 us -> 607 us
  starting transfers between devices: 22.7 us -> 46.7 us
    ppermute x0 -> x14, waiting for transfers between devices: none -> 75.3 us  [on_device(): part = lax.ppermute(part, 'expert', [(d, d ^ mask) for d in range(ways)])]
    all_to_all x1 -> x0, blocking collectives: 42.6 us -> none  [on_device(): lax.all_to_all(send_buffer, 'expert', split_axis=0, concat_axis=0, tiled=...]
    all_to_all x1, waiting for transfers between devices: 29.1 us -> 0.01 us  [on_device(): lax.all_to_all(grad_send, 'expert', split_axis=0, concat_axis=0, tiled=True)]
    ppermute x0 -> x14, starting transfers between devices: none -> 27.7 us  [on_device(): part = lax.ppermute(part, 'expert', [(d, d ^ mask) for d in range(ways)])]
    unnamed x262 -> x300, local copies, waits for them, and re-layouts: 32.4 us -> 34.8 us
  transfers between devices with their start and end apart: 15 -> 28, of which waited for: 14 -> 18; matrix products, arithmetic and copies ran while one was open for 13% -> 12% of each run, Pallas kernels for 0% -> 0%
where the time goes in v1:
time: 1220 us
  waiting for transfers between devices  607 us (50%)
  blocking collectives  206 us (17%)
  local copies, waits for them, and re-layouts  152 us (12%)
  matrix products  99.2 us (8%)
  other arithmetic  88.1 us (7%)
  starting transfers between devices  46.7 us (4%)
  between operations  16.8 us (1%)
    psum x1, waiting for transfers between devices, on_device(): lax.psum((stacked[2], stacked[3], stacked[4], stacked[5]), ('expert', 're...  118 us
    all_to_all x2, waiting for transfers between devices, on_device(): lax.all_to_all(expert_part, 'expert', split_axis=0, concat_axis=0, tiled=...  109 us
    ppermute x14, waiting for transfers between devices, on_device(): part = lax.ppermute(part, 'expert', [(d, d ^ mask) for d in range(ways)])  75.3 us
    psum x2, waiting for transfers between devices, on_device(): residual = residual + lax.psum(moe_part, 'tensor')  74.2 us
    all_to_all x1, blocking collectives, on_device(): lax.all_to_all(input_grad, 'expert', split_axis=0, concat_axis=0, tiled=T...  74.1 us
    psum x1, blocking collectives, on_device(): lax.psum((stacked[2], stacked[3], stacked[4], stacked[5]), ('expert', 're...  65.3 us
    all_to_all x1, waiting for transfers between devices, on_device(): lax.all_to_all(input_grad, 'expert', split_axis=0, concat_axis=0, tiled=T...  64 us
    psum x2, waiting for transfers between devices, on_device(): residual = residual + lax.psum(attn_part, 'tensor')  60.9 us
  transfers between devices with their start and end apart: 28, of which 18 were waited for; matrix products, arithmetic and copies ran while one was open for 12% of the time, Pallas kernels for 0%

profile of v1, /device:TPU:0, one launch (start us, length us, event | category | flops | bytes accessed | tf_op | source)
XLA Modules:
  0.0 1215.7 jit_solution(1305284106616068543)
XLA Ops:
  27.1 8.1 gather_fusion.5
  36.0 8.1 gather_fusion.7
  45.2 23.4 %all-reduce.14.cloned.1.call-done = f32[394,768]{1,0:T(8,128)} async-done(((f32[394,768]{1,0:T(8,128)}), f32[394,768]{1,0:T(8,128)}) %all-reduce.14.cloned.1.call-update) | async-done | bytes 1210384 | tf_op jit(solution)/shard_map/psum | solution.py:59
  73.3 6.1 scatter_custom_fusion
  88.0 4.2 collective-permute-start.2
  92.3 13.6 %collective-permute-done.2 = bf16[1,128,768]{2,1,0:T(8,128)(2,1)S(1)} collective-permute-done((bf16[1,128,768]{2,1,0:T(8,128)(2,1)S(1)}, bf16[1,128,768]{2,1,0:T(8,128)(2,1)S(1)}, u32[]{:S(2)}, u32[]{:S(2)}) %collective-permute-start.2) | collective-permute-done | bytes 196640 | tf_op jit(solution)/shard_map/ppermute | solution.py:84
  105.9 13.7 %collective-permute-done.3 = bf16[1,128,768]{2,1,0:T(8,128)(2,1)S(1)} collective-permute-done((bf16[1,128,768]{2,1,0:T(8,128)(2,1)S(1)}, bf16[1,128,768]{2,1,0:T(8,128)(2,1)S(1)}, u32[]{:S(2)}, u32[]{:S(2)}) %collective-permute-start.3) | collective-permute-done | bytes 196640 | tf_op jit(solution)/shard_map/ppermute | solution.py:84
  119.8 7.7 multiply_convert_fusion.1
  127.5 4.3 fusion.20
  131.8 4.8 all-to-all-start
  138.6 8.1 gather_fusion.4
  149.3 56.8 %all-to-all-done = f32[8,128,768]{2,1,0:T(8,128)S(1)} async-done(((f32[8,128,768]{2,1,0:T(8,128)}), f32[8,128,768]{2,1,0:T(8,128)S(1)}, u32[]{:S(2)}, u32[]{:S(2)}) %all-to-all-start) | async-done | bytes 3145760 | tf_op jit(solution)/shard_map/all_to_all | solution.py:95
  206.2 3.8 gather_fusion
  214.5 4.0 multiply_reduce_fusion.5
  218.7 42.0 %all-reduce.16.cloned.1.call-done = f32[394,768]{1,0:T(8,128)} async-done(((f32[394,768]{1,0:T(8,128)}), f32[394,768]{1,0:T(8,128)}) %all-reduce.16.cloned.1.call-update) | async-done | bytes 1210384 | tf_op jit(solution)/shard_map/psum | solution.py:98
  274.2 4.5 mul.501
  278.7 37.6 %all-reduce.18.cloned.1.call-done = f32[394,768]{1,0:T(8,128)} async-done(((f32[394,768]{1,0:T(8,128)}), f32[394,768]{1,0:T(8,128)}) %all-reduce.18.cloned.1.call-update) | async-done | bytes 1210384 | tf_op jit(solution)/shard_map/psum | solution.py:59
  319.5 8.1 gather_fusion.6
  329.6 8.8 scatter_custom_fusion.2
  338.4 5.5 all-to-all-start.2
  345.0 6.3 scatter_custom_fusion.1
  364.6 10.9 collective-permute-done.8
  375.5 4.2 collective-permute-start.10
  379.7 14.1 %collective-permute-done.9 = bf16[1,128,768]{2,1,0:T(8,128)(2,1)S(1)} collective-permute-done((bf16[1,128,768]{2,1,0:T(8,128)(2,1)S(1)}, bf16[1,128,768]{2,1,0:T(8,128)(2,1)S(1)}, u32[]{:S(2)}, u32[]{:S(2)}) %collective-permute-start.9) | collective-permute-done | bytes 196640 | tf_op jit(solution)/shard_map/ppermute | solution.py:84
  393.8 20.8 %collective-permute-done.10 = bf16[1,128,768]{2,1,0:T(8,128)(2,1)S(1)} collective-permute-done((bf16[1,128,768]{2,1,0:T(8,128)(2,1)S(1)}, bf16[1,128,768]{2,1,0:T(8,128)(2,1)S(1)}, u32[]{:S(2)}, u32[]{:S(2)}) %collective-permute-start.10) | collective-permute-done | bytes 196640 | tf_op jit(solution)/shard_map/ppermute | solution.py:84
  415.9 7.5 multiply_convert_fusion
  423.4 8.5 fusion.13
  433.6 4.3 fusion.16
  437.9 3.7 all-to-all-start.3
  441.5 6.9 fusion.18
  448.4 64.0 %all-to-all-done.3 = f32[8,128,768]{2,1,0:T(8,128)S(1)} async-done(((f32[8,128,768]{2,1,0:T(8,128)}), f32[8,128,768]{2,1,0:T(8,128)S(1)}, u32[]{:S(2)}, u32[]{:S(2)}) %all-to-all-start.3) | async-done | bytes 3145760 | tf_op jit(solution)/shard_map/all_to_all | solution.py:169
  514.1 3.7 all-to-all-start.1
  518.0 6.6 gather_fusion.2
  524.6 4.0 reshape.425
  528.6 5.6 reduce_sum.406
  536.5 52.1 %all-to-all-done.1 = f32[8,128,768]{2,1,0:T(8,128)S(1)} async-done(((f32[8,128,768]{2,1,0:T(8,128)}), f32[8,128,768]{2,1,0:T(8,128)S(1)}, u32[]{:S(2)}, u32[]{:S(2)}) %all-to-all-start.1) | async-done | bytes 3145760 | tf_op jit(solution)/shard_map/all_to_all | solution.py:95
  588.6 3.8 gather_fusion.1
  592.4 4.1 reshape.421
  596.6 8.1 multiply_reduce_fusion.3
  604.7 9.8 psum.103
  631.1 3.6 fusion.71
  635.1 42.9 %all-reduce.22.cloned.1.call-done = f32[394,768]{1,0:T(8,128)} async-done(((f32[394,768]{1,0:T(8,128)}), f32[394,768]{1,0:T(8,128)}) %all-reduce.22.cloned.1.call-update) | async-done | bytes 1210384 | tf_op jit(solution)/shard_map/psum | solution.py:243
  684.9 3.2 mul.539
  688.0 8.9 scatter_custom_fusion.3
  696.9 42.5 %all_to_all.30 = bf16[8,128,768]{2,1,0:T(8,128)(2,1)S(1)} all-to-all(bf16[8,128,768]{2,1,0:T(8,128)(2,1)} %bitcast.271), channel_id=1, replica_groups=mesh['tensor'=2,'expert'=8,'replica'=2] {'expert'}, dimensions={0} | all-to-all | bytes 3145728 | tf_op jit(solution)/shard_map/all_to_all | solution.py:148
  739.5 9.1 fusion.6
  751.3 74.1 %all_to_all.31 = f32[8,128,768]{2,1,0:T(8,128)S(1)} all-to-all(f32[8,128,768]{2,1,0:T(8,128)S(1)} %fusion.14), channel_id=1, replica_groups=mesh['tensor'=2,'expert'=8,'replica'=2] {'expert'}, dimensions={0} | all-to-all | bytes 6291456 | tf_op jit(solution)/shard_map/all_to_all | solution.py:169
  825.3 3.8 gather_fusion.3
  829.1 4.0 reshape.430
  833.1 5.7 reduce_sum.415
  842.1 14.5 %psum.106 = f32[394,2]{1,0:T(8,128)S(1)} all-reduce(f32[394,2]{1,0:T(8,128)S(1)} %multiply_reduce_fusion.2), channel_id=1, replica_groups=mesh['tensor'=2,'expert'=8,'replica'=2] {'tensor'}, use_global_device_ids=true, to_apply=%region_47.50 | all-reduce | flops 788 | bytes 6304 | tf_op jit(solution)/shard_map/psum | solution.py:174
  856.9 27.6 %all-reduce.24.cloned.1.call-done = f32[394,768]{1,0:T(8,128)} async-done(((f32[394,768]{1,0:T(8,128)}), f32[394,768]{1,0:T(8,128)}) %all-reduce.24.cloned.1.call-update) | async-done | bytes 1210384 | tf_op jit(solution)/shard_map/psum | solution.py:174
  899.3 3.9 fusion.68
  911.4 3.4 pad_maximum_fusion.2
  914.9 5.2 convolution_bitcast_fusion
  923.0 4.3 pad_maximum_fusion.1
  928.7 4.7 convolution_bitcast_fusion.2
  936.1 4.5 pad_maximum_fusion
  942.1 32.2 %all-reduce.28.cloned.1.call-done = (f32[394,768]{1,0:T(8,128)}, f32[394,768]{1,0:T(8,128)}) async-done(((f32[394,768]{1,0:T(8,128)}, f32[394,768]{1,0:T(8,128)}), (f32[394,768]{1,0:T(8,128)}, f32[394,768]{1,0:T(8,128)})) %all-reduce.28.cloned.1.call-update) | async-done | bytes 2420752 | tf_op jit(solution)/shard_map/psum | solution.py:98
  976.8 65.3 %all-reduce.2 = (f32[2,2,768]{2,1,0:T(2,128)}, f32[2,768,8]{1,2,0:T(8,128)}) all-reduce(f32[2,2,768]{2,1,0:T(2,128)S(1)} %pad_maximum_fusion.5, f32[2,768,8]{1,2,0:T(8,128)S(1)} %pad_maximum_fusion.4), channel_id=1, replica_groups=mesh['tensor'=2,'expert'=8,'replica'=2] {'expert','replica'}, use_global_device_ids=true, to_apply=%region_60.63 | all-reduce | flops 15360 | bytes 122880 | tf_op jit(solution)/shard_map/psum | solution.py:260
  1046.0 118.4 %all-reduce.26.cloned.1.call-done = (f32[2,3,768,384]{2,3,1,0:T(8,128)}, f32[2,384,768]{2,1,0:T(8,128)}) async-done(((f32[2,3,768,384]{2,3,1,0:T(8,128)}, f32[2,384,768]{2,1,0:T(8,128)}), (f32[2,3,768,384]{2,3,1,0:T(8,128)}, f32[2,384,768]{2,1,0:T(8,128)})) %all-reduce.26.cloned.1.call-update) | async-done | bytes 9437200 | tf_op jit(solution)/shard_map/psum | solution.py:260
  1164.3 8.2 copy.267
  1172.5 12.7 %reduce-scatter.5.cloned.1.call-done = f32[2,1536,384]{2,1,0:T(8,128)} async-done(((f32[2,1536,768]{2,1,0:T(8,128)}), f32[2,1536,384]{2,1,0:T(8,128)}) %reduce-scatter.5.cloned.1.call-update) | async-done | bytes 4718608 | tf_op jit(solution)/shard_map/reduce_scatter | solution.py:258
  1185.2 22.0 %reduce-scatter.3.cloned.1.call-done = f32[2,384,1536]{2,1,0:T(8,128)} async-done(((f32[2,768,1536]{2,1,0:T(8,128)}), f32[2,384,1536]{2,1,0:T(8,128)}) %reduce-scatter.3.cloned.1.call-update) | async-done | bytes 4718608 | tf_op jit(solution)/shard_map/reduce_scatter | solution.py:257
  (541 shorter events, 152.4 us)
Async XLA Ops:
  7.2 61.4 %all-reduce.14.cloned.1.call-start = ((), (), s32[]{:S(2)}) async-start(), calls=%async_computation.8 | async-start | bytes 2457600 | tf_op jit(solution)/shard_map/psum | solution.py:59
  11.3 59.1 %copy-start.88 = (f32[768]{0:T(1024)}, f32[768]{0:T(1024)S(1)}, u32[]{:S(2)}) copy-start(f32[768]{0:T(1024)S(1)} %get-tuple-element.61) | copy-start | bytes 9220
  21.9 22.3 %copy-start.38 = (s32[1,394,2]{2,1,0:T(8,128)}, s32[1,394,2]{2,1,0:T(8,128)S(1)}, u32[]{:S(2)}) copy-start(s32[1,394,2]{2,1,0:T(8,128)S(1)} %copy.307) | copy-start | bytes 9460
  36.0 32.6 %copy-start.14 = (bf16[394,768]{1,0:T(8,128)(2,1)S(1)}, bf16[394,768]{1,0:T(8,128)(2,1)}, u32[]{:S(2)}) copy-start(bf16[394,768]{1,0:T(8,128)(2,1)} %param.13) | copy-start | bytes 1815556
  45.2 91.4 %copy-start.134 = (s32[788]{0:T(1024)}, s32[788]{0:T(1024)S(1)}, u32[]{:S(2)}) copy-start(s32[788]{0:T(1024)S(1)} %get-tuple-element.124) | copy-start | bytes 9460
  79.5 48.0 %slice-start = ((s8[4718592]{0:T(1024)(128)(4,1)}), s8[4194304]{0:T(1024)(128)(4,1)S(1)}, s32[]{:S(2)}) async-start(s8[4718592]{0:T(1024)(128)(4,1)} %bitcast.280), calls=%async_computation.18 | async-start | bytes 8388608
  79.6 8.4 collective-permute-start
  81.2 11.0 collective-permute-start.1
  82.6 37.1 %collective-permute-start.6 = (bf16[1,128,768]{2,1,0:T(8,128)(2,1)S(1)}, bf16[1,128,768]{2,1,0:T(8,128)(2,1)S(1)}, u32[]{:S(2)}, u32[]{:S(2)}) collective-permute-start(bf16[1,128,768]{2,1,0:T(8,128)(2,1)S(1)} %get-tuple-element.90), channel_id=1, source_target_pairs={{0,14},{2,12},{4,10},{6,8},{8,6},{10,4},{12,2},{14,0},{1,15},{3,13... | collective-permute-start | bytes 589832 | tf_op jit(solution)/shard_map/ppermute | solution.py:84
  85.0 34.7 %collective-permute-start.5 = (bf16[1,128,768]{2,1,0:T(8,128)(2,1)S(1)}, bf16[1,128,768]{2,1,0:T(8,128)(2,1)S(1)}, u32[]{:S(2)}, u32[]{:S(2)}) collective-permute-start(bf16[1,128,768]{2,1,0:T(8,128)(2,1)S(1)} %get-tuple-element.91), channel_id=1, source_target_pairs={{0,12},{2,14},{4,8},{6,10},{8,4},{10,6},{12,0},{14,2},{1,13},{3,15... | collective-permute-start | bytes 589832 | tf_op jit(solution)/shard_map/ppermute | solution.py:84
  86.5 33.2 %collective-permute-start.4 = (bf16[1,128,768]{2,1,0:T(8,128)(2,1)S(1)}, bf16[1,128,768]{2,1,0:T(8,128)(2,1)S(1)}, u32[]{:S(2)}, u32[]{:S(2)}) collective-permute-start(bf16[1,128,768]{2,1,0:T(8,128)(2,1)S(1)} %get-tuple-element.92), channel_id=1, source_target_pairs={{0,10},{2,8},{4,14},{6,12},{8,2},{10,0},{12,6},{14,4},{1,11},{3,9}... | collective-permute-start | bytes 589832 | tf_op jit(solution)/shard_map/ppermute | solution.py:84
  88.0 17.9 %collective-permute-start.2 = (bf16[1,128,768]{2,1,0:T(8,128)(2,1)S(1)}, bf16[1,128,768]{2,1,0:T(8,128)(2,1)S(1)}, u32[]{:S(2)}, u32[]{:S(2)}) collective-permute-start(bf16[1,128,768]{2,1,0:T(8,128)(2,1)S(1)} %get-tuple-element.94), channel_id=1, source_target_pairs={{0,6},{2,4},{4,2},{6,0},{8,14},{10,12},{12,10},{14,8},{1,7},{3,5},... | collective-permute-start | bytes 589832 | tf_op jit(solution)/shard_map/ppermute | solution.py:84
  92.2 27.4 %collective-permute-start.3 = (bf16[1,128,768]{2,1,0:T(8,128)(2,1)S(1)}, bf16[1,128,768]{2,1,0:T(8,128)(2,1)S(1)}, u32[]{:S(2)}, u32[]{:S(2)}) collective-permute-start(bf16[1,128,768]{2,1,0:T(8,128)(2,1)S(1)} %get-tuple-element.93), channel_id=1, source_target_pairs={{0,8},{2,10},{4,12},{6,14},{8,0},{10,2},{12,4},{14,6},{1,9},{3,11}... | collective-permute-start | bytes 589832 | tf_op jit(solution)/shard_map/ppermute | solution.py:84
  131.8 74.4 %all-to-all-start = ((f32[8,128,768]{2,1,0:T(8,128)}), f32[8,128,768]{2,1,0:T(8,128)S(1)}, u32[]{:S(2)}, u32[]{:S(2)}) async-start(f32[8,128,768]{2,1,0:T(8,128)} %fusion.20), calls=%async_computation | async-start | bytes 6291456 | tf_op jit(solution)/shard_map/all_to_all | solution.py:95
  136.5 124.2 %all-reduce.16.cloned.1.call-start = ((), (), s32[]{:S(2)}) async-start(), calls=%async_computation.9 | async-start | bytes 2457600 | tf_op jit(solution)/shard_map/psum | solution.py:98
  136.6 69.5 %copy-start.108 = (s32[1024]{0:T(1024)}, s32[1024]{0:T(1024)S(1)}, u32[]{:S(2)}) copy-start(s32[1024]{0:T(1024)S(1)} %pad_clamp_fusion.1) | copy-start | bytes 12292
  218.4 42.3 %copy-start.6 = (f32[394,768]{1,0:T(8,128)S(1)}, f32[394,768]{1,0:T(8,128)}, u32[]{:S(2)}) copy-start(f32[394,768]{1,0:T(8,128)} %copy-done.5) | copy-start | bytes 3631108
  218.5 45.0 %copy-start.86 = (f32[768]{0:T(1024)S(1)}, f32[768]{0:T(1024)}, u32[]{:S(2)}) copy-start(f32[768]{0:T(1024)} %get-tuple-element.63) | copy-start | bytes 9220
  218.5 97.8 %all-reduce.18.cloned.1.call-start = ((), (), s32[]{:S(2)}) async-start(), calls=%async_computation.10 | async-start | bytes 2457600 | tf_op jit(solution)/shard_map/psum | solution.py:59
  262.4 53.9 %copy-start.11 = (f32[394,768]{1,0:T(8,128)}, f32[394,768]{1,0:T(8,128)S(1)}, u32[]{:S(2)}) copy-start(f32[394,768]{1,0:T(8,128)S(1)} %get-tuple-element.79) | copy-start | bytes 3631108
  278.7 39.5 %copy-start.90 = (f32[768]{0:T(1024)S(1)}, f32[768]{0:T(1024)}, u32[]{:S(2)}) copy-start(f32[768]{0:T(1024)} %get-tuple-element.60) | copy-start | bytes 9220
  318.4 25.5 %copy-start.31 = (bf16[394,768]{1,0:T(8,128)(2,1)}, bf16[394,768]{1,0:T(8,128)(2,1)S(1)}, u32[]{:S(2)}) copy-start(bf16[394,768]{1,0:T(8,128)(2,1)S(1)} %multiply_convert_fusion.6) | copy-start | bytes 1815556
  338.4 85.0 %all-to-all-start.2 = ((bf16[8,128,768]{2,1,0:T(8,128)(2,1)}), bf16[8,128,768]{2,1,0:T(8,128)(2,1)}, u32[]{:S(2)}, u32[]{:S(2)}) async-start(bf16[8,128,768]{2,1,0:T(8,128)(2,1)} %bitcast.264), calls=%async_computation.2 | async-start | bytes 3145728 | tf_op jit(solution)/shard_map/all_to_all | solution.py:148
  351.5 11.0 collective-permute-start.7
  353.6 21.9 %collective-permute-start.8 = (bf16[1,128,768]{2,1,0:T(8,128)(2,1)S(1)}, bf16[1,128,768]{2,1,0:T(8,128)(2,1)S(1)}, u32[]{:S(2)}, u32[]{:S(2)}) collective-permute-start(bf16[1,128,768]{2,1,0:T(8,128)(2,1)S(1)} %get-tuple-element.87), channel_id=1, source_target_pairs={{0,4},{2,6},{4,0},{6,2},{8,12},{10,14},{12,8},{14,10},{1,5},{3,7},... | collective-permute-start | bytes 589832 | tf_op jit(solution)/shard_map/ppermute | solution.py:84
  355.1 59.7 %collective-permute-start.13 = (bf16[1,128,768]{2,1,0:T(8,128)(2,1)S(1)}, bf16[1,128,768]{2,1,0:T(8,128)(2,1)S(1)}, u32[]{:S(2)}, u32[]{:S(2)}) collective-permute-start(bf16[1,128,768]{2,1,0:T(8,128)(2,1)S(1)} %get-tuple-element.82), channel_id=1, source_target_pairs={{0,14},{2,12},{4,10},{6,8},{8,6},{10,4},{12,2},{14,0},{1,15},{3,13... | collective-permute-start | bytes 589832 | tf_op jit(solution)/shard_map/ppermute | solution.py:84
  357.5 57.3 %collective-permute-start.12 = (bf16[1,128,768]{2,1,0:T(8,128)(2,1)S(1)}, bf16[1,128,768]{2,1,0:T(8,128)(2,1)S(1)}, u32[]{:S(2)}, u32[]{:S(2)}) collective-permute-start(bf16[1,128,768]{2,1,0:T(8,128)(2,1)S(1)} %get-tuple-element.83), channel_id=1, source_target_pairs={{0,12},{2,14},{4,8},{6,10},{8,4},{10,6},{12,0},{14,2},{1,13},{3,15... | collective-permute-start | bytes 589832 | tf_op jit(solution)/shard_map/ppermute | solution.py:84
  358.9 55.8 %collective-permute-start.11 = (bf16[1,128,768]{2,1,0:T(8,128)(2,1)S(1)}, bf16[1,128,768]{2,1,0:T(8,128)(2,1)S(1)}, u32[]{:S(2)}, u32[]{:S(2)}) collective-permute-start(bf16[1,128,768]{2,1,0:T(8,128)(2,1)S(1)} %get-tuple-element.84), channel_id=1, source_target_pairs={{0,10},{2,8},{4,14},{6,12},{8,2},{10,0},{12,6},{14,4},{1,11},{3,9}... | collective-permute-start | bytes 589832 | tf_op jit(solution)/shard_map/ppermute | solution.py:84
  362.5 31.2 %collective-permute-start.9 = (bf16[1,128,768]{2,1,0:T(8,128)(2,1)S(1)}, bf16[1,128,768]{2,1,0:T(8,128)(2,1)S(1)}, u32[]{:S(2)}, u32[]{:S(2)}) collective-permute-start(bf16[1,128,768]{2,1,0:T(8,128)(2,1)S(1)} %get-tuple-element.86), channel_id=1, source_target_pairs={{0,6},{2,4},{4,2},{6,0},{8,14},{10,12},{12,10},{14,8},{1,7},{3,5},... | collective-permute-start | bytes 589832 | tf_op jit(solution)/shard_map/ppermute | solution.py:84
  375.5 39.1 %collective-permute-start.10 = (bf16[1,128,768]{2,1,0:T(8,128)(2,1)S(1)}, bf16[1,128,768]{2,1,0:T(8,128)(2,1)S(1)}, u32[]{:S(2)}, u32[]{:S(2)}) collective-permute-start(bf16[1,128,768]{2,1,0:T(8,128)(2,1)S(1)} %get-tuple-element.85), channel_id=1, source_target_pairs={{0,8},{2,10},{4,12},{6,14},{8,0},{10,2},{12,4},{14,6},{1,9},{3,11}... | collective-permute-start | bytes 589832 | tf_op jit(solution)/shard_map/ppermute | solution.py:84
  437.9 74.6 %all-to-all-start.3 = ((f32[8,128,768]{2,1,0:T(8,128)}), f32[8,128,768]{2,1,0:T(8,128)S(1)}, u32[]{:S(2)}, u32[]{:S(2)}) async-start(f32[8,128,768]{2,1,0:T(8,128)} %fusion.16), calls=%async_computation.3 | async-start | bytes 6291456 | tf_op jit(solution)/shard_map/all_to_all | solution.py:169
  514.1 74.5 %all-to-all-start.1 = ((f32[8,128,768]{2,1,0:T(8,128)}), f32[8,128,768]{2,1,0:T(8,128)S(1)}, u32[]{:S(2)}, u32[]{:S(2)}) async-start(f32[8,128,768]{2,1,0:T(8,128)} %fusion.18), calls=%async_computation.1 | async-start | bytes 6291456 | tf_op jit(solution)/shard_map/all_to_all | solution.py:95
  517.7 97.0 %all-reduce.20.cloned.1.call-start = ((), (), s32[]{:S(2)}) async-start(), calls=%async_computation.11 | async-start | bytes 2457600 | tf_op jit(solution)/shard_map/psum | solution.py:174
  534.2 143.7 %all-reduce.22.cloned.1.call-start = ((), (), s32[]{:S(2)}) async-start(), calls=%async_computation.12 | async-start | bytes 2457600 | tf_op jit(solution)/shard_map/psum | solution.py:243
  596.5 18.1 %copy-start.107 = (s32[394,2]{0,1:T(2,128)S(1)}, s32[394,2]{0,1:T(2,128)}, u32[]{:S(2)}) copy-start(s32[394,2]{0,1:T(2,128)} %copy-done.106) | copy-start | bytes 9460
  596.5 18.1 %copy-start.103 = (f32[394]{0:T(512)S(1)}, f32[394]{0:T(512)}, u32[]{:S(2)}) copy-start(f32[394]{0:T(512)} %copy-done.102) | copy-start | bytes 4732
  596.5 18.1 %copy-start.122 = (f32[394]{0:T(512)S(1)}, f32[394]{0:T(512)}, u32[]{:S(2)}) copy-start(f32[394]{0:T(512)} %copy-done.121) | copy-start | bytes 4732
  596.5 18.2 %copy-start.9 = (f32[394,768]{1,0:T(8,128)S(1)}, f32[394,768]{1,0:T(8,128)}, u32[]{:S(2)}) copy-start(f32[394,768]{1,0:T(8,128)} %copy-done.8) | copy-start | bytes 3631108
  596.5 18.2 %copy-start.91 = (f32[768]{0:T(1024)S(1)}, f32[768]{0:T(1024)}, u32[]{:S(2)}) copy-start(f32[768]{0:T(1024)} %get-tuple-element.60) | copy-start | bytes 9220
  596.5 18.2 %copy-start.99 = (f32[394]{0:T(512)S(1)}, f32[394]{0:T(512)}, u32[]{:S(2)}) copy-start(f32[394]{0:T(512)} %copy-done.98) | copy-start | bytes 4732
  596.5 18.2 %copy-start.117 = (f32[394]{0:T(512)S(1)}, f32[394]{0:T(512)}, u32[]{:S(2)}) copy-start(f32[394]{0:T(512)} %copy-done.116) | copy-start | bytes 4732
  618.0 62.5 %copy-start.110 = (f32[394]{0:T(512)}, f32[394]{0:T(512)S(1)}, u32[]{:S(2)}) copy-start(f32[394]{0:T(512)S(1)} %negate_multiply_fusion.3) | copy-start | bytes 4732
  631.1 46.9 %copy-start.87 = (f32[768]{0:T(1024)S(1)}, f32[768]{0:T(1024)}, u32[]{:S(2)}) copy-start(f32[768]{0:T(1024)} %get-tuple-element.63) | copy-start | bytes 9220
  631.1 46.9 %copy-start.95 = (f32[394]{0:T(512)S(1)}, f32[394]{0:T(512)}, u32[]{:S(2)}) copy-start(f32[394]{0:T(512)} %copy-done.94) | copy-start | bytes 4732
  631.1 46.9 %copy-start.113 = (f32[394]{0:T(512)S(1)}, f32[394]{0:T(512)}, u32[]{:S(2)}) copy-start(f32[394]{0:T(512)} %copy-done.112) | copy-start | bytes 4732
  634.6 43.4 %copy-start.12 = (f32[394,768]{1,0:T(8,128)S(1)}, f32[394,768]{1,0:T(8,128)}, u32[]{:S(2)}) copy-start(f32[394,768]{1,0:T(8,128)} %copy-done.11) | copy-start | bytes 3631108
  634.7 45.2 %copy-start.130 = (f32[394]{0:T(512)S(1)}, f32[394]{0:T(512)}, u32[]{:S(2)}) copy-start(f32[394]{0:T(512)} %copy-done.129) | copy-start | bytes 4732
  634.7 249.8 %all-reduce.24.cloned.1.call-start = ((), (), s32[]{:S(2)}) async-start(), calls=%async_computation.13 | async-start | bytes 2457600 | tf_op jit(solution)/shard_map/psum | solution.py:174
  688.0 60.6 %slice-start.4 = ((s8[4718592]{0:T(1024)(128)(4,1)}), s8[524288]{0:T(1024)(128)(4,1)S(1)}, s32[]{:S(2)}) async-start(s8[4718592]{0:T(1024)(128)(4,1)} %bitcast.284), calls=%async_computation.22 | async-start | bytes 1048576
  751.3 74.1 %copy-start.109 = (s32[1024]{0:T(1024)S(1)}, s32[1024]{0:T(1024)}, u32[]{:S(2)}) copy-start(s32[1024]{0:T(1024)} %copy-done.108) | copy-start | bytes 12292
  838.8 135.4 %all-reduce.28.cloned.1.call-start = ((), (), s32[]{:S(2)}) async-start(), calls=%async_computation.17 | async-start | bytes 4915200 | tf_op jit(solution)/shard_map/psum | solution.py:98
  838.9 17.9 %copy-start.74 = (f32[394,8]{0,1:T(8,128)S(1)}, f32[394,8]{0,1:T(8,128)}, u32[]{:S(2)}) copy-start(f32[394,8]{0,1:T(8,128)} %copy-done.73) | copy-start | bytes 37828
  839.0 17.9 %copy-start.101 = (f32[394]{0:T(512)S(1)}, f32[394]{0:T(512)}, u32[]{:S(2)}) copy-start(f32[394]{0:T(512)} %copy-done.100) | copy-start | bytes 4732
  839.0 45.5 %copy-start.7 = (f32[394,768]{1,0:T(8,128)S(1)}, f32[394,768]{1,0:T(8,128)}, u32[]{:S(2)}) copy-start(f32[394,768]{1,0:T(8,128)} %copy-done.5) | copy-start | bytes 3631108
  839.0 45.5 %copy-start.89 = (f32[768]{0:T(1024)S(1)}, f32[768]{0:T(1024)}, u32[]{:S(2)}) copy-start(f32[768]{0:T(1024)} %copy-done.88) | copy-start | bytes 9220
  839.0 45.5 %copy-start.97 = (f32[394]{0:T(512)S(1)}, f32[394]{0:T(512)}, u32[]{:S(2)}) copy-start(f32[394]{0:T(512)} %copy-done.96) | copy-start | bytes 4732
  839.0 45.5 %copy-start.115 = (f32[394]{0:T(512)S(1)}, f32[394]{0:T(512)}, u32[]{:S(2)}) copy-start(f32[394]{0:T(512)} %copy-done.114) | copy-start | bytes 4732
  856.9 29.5 %copy-start.128 = (f32[394]{0:T(512)S(1)}, f32[394]{0:T(512)}, u32[]{:S(2)}) copy-start(f32[394]{0:T(512)} %copy-done.127) | copy-start | bytes 4732
  903.2 261.2 %all-reduce.26.cloned.1.call-start = ((), (), s32[]{:S(2)}) async-start(), calls=%async_computation.16 | async-start | bytes 18874368 | tf_op jit(solution)/shard_map/psum | solution.py:260
  914.9 270.3 %reduce-scatter.5.cloned.1.call-start = ((), (), s32[]{:S(2)}) async-start(), calls=%async_computation.15 | async-start | bytes 14155776 | tf_op jit(solution)/shard_map/reduce_scatter | solution.py:258
  927.3 279.9 %reduce-scatter.3.cloned.1.call-start = ((), (), s32[]{:S(2)}) async-start(), calls=%async_computation.14 | async-start | bytes 14155776 | tf_op jit(solution)/shard_map/reduce_scatter | solution.py:257
  941.6 34.5 %copy-start.126 = (f32[394]{0:T(512)S(1)}, f32[394]{0:T(512)}, u32[]{:S(2)}) copy-start(f32[394]{0:T(512)} %copy-done.125) | copy-start | bytes 4732
  974.3 67.9 %copy-start.10 = (f32[394,768]{1,0:T(8,128)S(1)}, f32[394,768]{1,0:T(8,128)}, u32[]{:S(2)}) copy-start(f32[394,768]{1,0:T(8,128)} %copy-done.8) | copy-start | bytes 3631108
  1164.3 42.9 %copy-start.61 = (f32[2,384,768]{2,1,0:T(8,128)S(1)}, f32[2,384,768]{2,1,0:T(8,128)}, u32[]{:S(2)}) copy-start(f32[2,384,768]{2,1,0:T(8,128)} %get-tuple-element.130) | copy-start | bytes 7077892
  (110 other events, 334.5 us)
Sparse Core Ops, SparseCore 0:
  21.8 46.6 all-reduce.13
  218.6 42.0 all-reduce.15
  272.3 43.9 all-reduce.17
  534.4 44.3 all-reduce.19
  634.8 43.1 all-reduce.21
  839.0 45.4 all-reduce.23
  903.3 70.9 all-reduce.27
  978.6 185.7 all-reduce.25
  1167.3 17.8 reduce-scatter.4
  1188.0 19.1 reduce-scatter.2
